TPU v7x, 128 devices: a whole 4x4x4 slice. The times are simulated.
128 devices in a mesh: grp: 32 (over y, x, core), own: 4 (over z).
Axes of the slice: x: 4, y: 4, z: 4, core: 2. Of those that a mesh axis runs over, the one named last changes fastest.
Arguments:
- background: bfloat16 [256, 1024, 512], P('grp', 'own'), may hold values from -6 to 6
- obs_ens: bfloat16 [256, 2048, 512], P('grp', 'own'), may hold values from -12 to 12
- innovation: bfloat16 [256, 2048], P('grp', 'own'), may hold values from -6 to 6
- obs_weight: bfloat16 [256, 2048], P('grp', 'own'), may hold values from 0.25 to 4
- obs_count: int32 [256, 4], P('grp', 'own'), may hold values from 128 to 512, as said below
- dest: int32 [256], replicated, may hold values from 0 to 31, as said below
Outputs:
- analysis: bfloat16 [256, 1024, 512], P('grp', 'own')
Inputs may be any that keep to these rules, and one draw needn't show every extreme that they name: `obs_count`: each entry counts the live leading slots of one owner's block of 512; later slots carry values that must be ignored. The largest entry of every draw equals 512. `dest`: every index of grp is named by exactly 8 groups, and no two groups of one index of grp name the same index.
All inputs are finite; a program needn't handle non-finite values.
Results may differ from a plain program's by a relative error of at most 0.012.
The roundings to bfloat16 on the way count: a program that leaves them out, or rounds other values in their place, can miss the bound.
Values may be sent and summed in bfloat16 or wider, within the bound.
A program may use at most 128 MiB of HBM per device.

v0:
```python
import jax
import jax.numpy as jnp
from jax import lax
from jax.sharding import PartitionSpec as P

NS_IT = 4


def newton_weights(gram, right_side):
    members = gram.shape[-1]
    eye_mat = jnp.eye(members, dtype=jnp.float32)
    matrix = gram + (members - 1.0) * eye_mat
    norm_scale = jnp.sqrt(jnp.sum(matrix * matrix, axis=(1, 2)))
    root_iter = (matrix / norm_scale[:, None, None]).astype(jnp.bfloat16)
    inverse = jnp.broadcast_to(eye_mat.astype(jnp.bfloat16), matrix.shape)
    for iteration in range(NS_IT):
        product = jnp.einsum("gij,gjk->gik", inverse, root_iter, preferred_element_type=jnp.float32)
        factor = (1.5 * eye_mat - 0.5 * product).astype(jnp.bfloat16)
        root_iter = jnp.einsum(
            "gij,gjk->gik", root_iter, factor, preferred_element_type=jnp.float32
        ).astype(jnp.bfloat16)
        inverse = jnp.einsum(
            "gij,gjk->gik", factor, inverse, preferred_element_type=jnp.float32
        ).astype(jnp.bfloat16)
    inverse_wide = inverse.astype(jnp.float32)
    half_way = jnp.einsum("gij,gj->gi", inverse_wide, right_side)
    mean_weight = jnp.einsum("gij,gj->gi", inverse_wide, half_way) / norm_scale[:, None]
    weights = (
        jnp.sqrt((members - 1.0) / norm_scale)[:, None, None] * inverse_wide
        + mean_weight[:, :, None]
    )
    return weights.astype(jnp.bfloat16)


def solve_weights(obs_pert, weight, source):
    weighted = (obs_pert.astype(jnp.float32) * weight.astype(jnp.float32)[:, :, None]).astype(
        jnp.bfloat16
    )
    gram_local = jnp.einsum("gpk,gpl->gkl", weighted, obs_pert, preferred_element_type=jnp.float32)
    right_local = jnp.einsum("gp,gpk->gk", source, obs_pert, preferred_element_type=jnp.float32)
    gram_part, right_part = (
        lax.psum_scatter(gram_local, "own", scatter_dimension=0, tiled=True),
        lax.psum_scatter(right_local, "own", scatter_dimension=0, tiled=True),
    )
    return lax.all_gather(newton_weights(gram_part, right_part), "own", axis=0, tiled=True)


def apply_weights(state_here, weights):
    state_mean = jnp.mean(state_here.astype(jnp.float32), axis=2, keepdims=True)
    state_pert = (state_here.astype(jnp.float32) - state_mean).astype(jnp.bfloat16)
    result = state_mean + jnp.einsum(
        "grk,gkl->grl", state_pert, weights, preferred_element_type=jnp.float32
    )
    return result.astype(jnp.bfloat16)


def pack_rows(array_in, send_index, send_live):
    picked = jnp.take(array_in, send_index, axis=0)
    keep_mask = send_live.reshape((-1,) + (1,) * (array_in.ndim - 1))
    return jnp.where(keep_mask, picked, jnp.zeros_like(picked))


def body(background, obs_ens, innovation, obs_weight, obs_count, dest):
    grp_size = lax.axis_size("grp")
    grp_index = lax.axis_index("grp")
    local_groups = background.shape[0]
    obs_rows = obs_ens.shape[1]
    obs_mean = jnp.mean(obs_ens.astype(jnp.float32), axis=2, keepdims=True)
    obs_pert = (obs_ens.astype(jnp.float32) - obs_mean).astype(jnp.bfloat16)
    position_in = lax.broadcasted_iota(jnp.int32, (local_groups, obs_rows), 1)
    live_rows = position_in < obs_count
    weight = jnp.where(live_rows, obs_weight, jnp.zeros_like(obs_weight))
    source = (weight.astype(jnp.float32) * innovation.astype(jnp.float32)).astype(jnp.bfloat16)
    group_total = dest.shape[0]
    group_ids = jnp.arange(group_total, dtype=jnp.int32)
    same_dest = dest[None, :] == dest[:, None]
    earlier = group_ids[None, :] < group_ids[:, None]
    arrival_rank = jnp.sum(jnp.where(same_dest & earlier, 1, 0), axis=1).astype(jnp.int32)
    my_dest = lax.dynamic_slice_in_dim(dest, grp_index * local_groups, local_groups)
    peer_ids = jnp.arange(grp_size, dtype=jnp.int32)
    local_ids = jnp.arange(local_groups, dtype=jnp.int32)
    peer_hits = my_dest[None, :] == peer_ids[:, None]
    send_index = jnp.sum(jnp.where(peer_hits, local_ids[None, :], 0), axis=1)
    send_live = jnp.any(peer_hits, axis=1)
    arriving = (dest[None, :] == grp_index) & (arrival_rank[None, :] == local_ids[:, None])
    arrive_group = jnp.sum(jnp.where(arriving, group_ids[None, :], 0), axis=1)
    arrive_source = arrive_group // local_groups
    weights = solve_weights(obs_pert, weight, source)
    result = apply_weights(background, weights)
    return jnp.take(
        lax.all_to_all(
            pack_rows(result, send_index, send_live), "grp", split_axis=0, concat_axis=0, tiled=True
        ),
        arrive_source,
        axis=0,
    )


def solution(mesh):
    return jax.shard_map(
        body,
        mesh=mesh,
        in_specs=(
            P("grp", "own", None),
            P("grp", "own", None),
            P("grp", "own"),
            P("grp", "own"),
            P("grp", "own"),
            P(),
        ),
        out_specs=P("grp", "own", None),
        check_vma=False,
    )
```

profile of v0, /device:TPU:0, one launch (start us, length us, event | category | flops | bytes accessed | tf_op | source)
XLA Modules:
  0.0 308.9 jit_solution(16136951597792057878)
XLA Ops:
  6.5 3.0 convert_reduce_fusion
  10.0 6.3 %fusion.1 = f32[8,512,512]{2,1,0:T(8,128)} fusion(f32[8,512]{1,0:T(8,128)S(1)} %fusion.16, bf16[8,512,512]{2,1,0:T(8,128)(2,1)S(1)} %copy-done, f32[8,512]{1,0:T(8,128)S(1)} %broadcast_multiply_fusion), kind=kOutput, calls=%fused_computation.7 | convolution fusion | flops 2166358016 | bytes 12615680 | tf_op jit(solution)/shard_map/gpk,gpl->gkl/dot_general | solution.py:39
  17.1 2.8 fusion.5
  21.1 19.0 %all-reduce = bf16[8,512]{1,0:T(8,128)(2,1)S(1)} all-reduce(f32[8,512]{1,0:T(8,128)S(1)} %bitcast.53), channel_id=3, replica_groups=mesh['grp'=32,'own'=4] {'own'}, use_global_device_ids=true, to_apply=%region_8.9.clone | all-reduce | flops 4096 | bytes 24576
  40.4 59.6 %reduce-scatter.2.cloned.1.call-done = f32[2,512,512]{2,1,0:T(8,128)} async-done(((f32[8,512,512]{2,1,0:T(8,128)}), f32[2,512,512]{2,1,0:T(8,128)}) %reduce-scatter.2.cloned.1.call-update) | async-done | bytes 2097168 | tf_op jit(solution)/shard_map/reduce_scatter | solution.py:42
  100.0 2.1 multiply_reduce_fusion
  102.8 0.7 subtract_convert_fusion.3
  103.5 0.7 convolution_convert_fusion.5
  104.2 0.7 convolution_convert_fusion.6
  105.0 0.7 subtract_convert_fusion.2
  107.1 0.7 subtract_convert_fusion.1
  107.9 1.0 copy-done.8
  108.9 1.7 convolution_convert_fusion.2
  110.5 3.8 %subtract_convert_fusion = bf16[2,512,512]{2,1,0:T(8,128)(2,1)} fusion(bf16[2,512,512]{2,1,0:T(8,128)(2,1)} %convolution_convert_fusion.2, bf16[2,512,512]{2,1,0:T(8,128)(2,1)S(1)} %convolution_convert_fusion.3, bf16[2,512,512]{2,1,0:T(8,128)(2,1)} %copy-done.8, f32[512,512]{1,0:T(8,128)S(1)} %fusion.9), kind=kOutput, calls=%fused_computation.15 | convolution fusion | flops 1075838976 | bytes 5242880 | tf_op jit(solution)/shard_map/gij,gjk->gik/dot_general | solution.py:17
  114.4 2.2 convolution_convert_fusion
  117.5 1.3 add_convert_fusion.1
  119.5 47.3 %all-gather.2.cloned.1.call-done = bf16[8,512,512]{2,1,0:T(8,128)(2,1)} async-done(((bf16[2,512,512]{2,1,0:T(8,128)(2,1)}), bf16[8,512,512]{2,1,0:T(8,128)(2,1)}) %all-gather.2.cloned.1.call-update) | async-done | bytes 4194320 | tf_op jit(solution)/shard_map/all_gather | solution.py:45
  166.8 4.1 %add_convert_fusion = bf16[8,256,512]{2,1,0:T(8,128)(2,1)S(1)} fusion(bf16[8,512,512]{2,1,0:T(8,128)(2,1)} %all-gather.2.cloned.1.call-done, bf16[8,256,512]{2,1,0:T(8,128)(2,1)} %param.6, f32[8,256]{1,0:T(8,128)S(1)} %broadcast_multiply_fusion.1), kind=kOutput, calls=%fused_computation.11 | convolution fusion | flops 1078984704 | bytes 8396800 | tf_op jit(solution)/shard_map/grk,gkl->grl/dot_general | solution.py:51
  170.9 4.8 %gather_fusion = bf16[32,256,512]{2,1,0:T(8,128)(2,1)} fusion(bf16[8,256,512]{2,1,0:T(8,128)(2,1)S(1)} %add_convert_fusion, s32[1024]{0:T(1024)S(1)} %pad_clamp_fusion.1), kind=kCustom, calls=%fused_computation | custom fusion | bytes 16777344 | tf_op jit(solution)/shard_map/jit(_take)/gather | solution.py:58
  175.8 7.6 %select_select_fusion = bf16[32,256,512]{2,1,0:T(8,128)(2,1)} fusion(bf16[32,256,512]{2,1,0:T(8,128)(2,1)} %gather_fusion, pred[32]{0:T(512)(128)(4,1)S(1)} %compare_and_fusion, pred[32]{0:T(512)(128)(4,1)S(1)} %fusion.23), kind=kLoop, calls=%fused_computation.5 | loop fusion | flops 8388608 | bytes 16777280 | tf_op jit(solution)/shard_map/jit(_where)/select_n | solution.py:60
  183.3 7.2 %all-to-all-start = ((bf16[32,256,512]{2,1,0:T(8,128)(2,1)}), bf16[32,256,512]{2,1,0:T(8,128)(2,1)}, u32[]{:S(2)}, u32[]{:S(2)}) async-start(bf16[32,256,512]{2,1,0:T(8,128)(2,1)} %select_select_fusion), calls=%async_computation.1 | async-start | bytes 16777216 | tf_op jit(solution)/shard_map/all_to_all | solution.py:91
  190.9 105.5 %all-to-all-done = bf16[32,256,512]{2,1,0:T(8,128)(2,1)} async-done(((bf16[32,256,512]{2,1,0:T(8,128)(2,1)}), bf16[32,256,512]{2,1,0:T(8,128)(2,1)}, u32[]{:S(2)}, u32[]{:S(2)}) %all-to-all-start) | async-done | bytes 8388640 | tf_op jit(solution)/shard_map/all_to_all | solution.py:91
  296.4 4.1 %gather_fusion.1 = bf16[8,256,512]{2,1,0:T(8,128)(2,1)S(1)} fusion(bf16[32,256,512]{2,1,0:T(8,128)(2,1)} %all-to-all-done, s32[1024]{0:T(1024)S(1)} %pad_clamp_fusion), kind=kCustom, calls=%fused_computation.1 | custom fusion | bytes 4194336 | tf_op jit(solution)/shard_map/jit(_take)/gather | solution.py:90
  300.5 1.6 broadcast_select_fusion
  (52 shorter events, 6.0 us)
Async XLA Ops:
  6.5 3.0 copy-start.6
  6.5 3.0 copy-start.3
  6.5 93.5 %reduce-scatter.2.cloned.1.call-start = ((), (), s32[]{:S(2)}) async-start(), calls=%async_computation.2 | async-start | bytes 10485760 | tf_op jit(solution)/shard_map/reduce_scatter | solution.py:42
  6.5 3.5 %copy-start = (bf16[8,512,512]{2,1,0:T(8,128)(2,1)S(1)}, bf16[8,512,512]{2,1,0:T(8,128)(2,1)}, u32[]{:S(2)}) copy-start(bf16[8,512,512]{2,1,0:T(8,128)(2,1)} %param.7) | copy-start | bytes 12582916
  16.3 0.7 copy-start.5
  16.3 150.4 %all-gather.2.cloned.1.call-start = ((), (), s32[]{:S(2)}) async-start(), calls=%async_computation.3 | async-start | bytes 5242880 | tf_op jit(solution)/shard_map/all_gather | solution.py:45
  17.1 2.8 copy-start.7
  100.0 2.2 copy-start.1
  107.9 1.0 copy-start.8
  117.0 1.8 copy-start.4
  117.0 2.1 copy-start.2
  183.3 113.1 %all-to-all-start = ((bf16[32,256,512]{2,1,0:T(8,128)(2,1)}), bf16[32,256,512]{2,1,0:T(8,128)(2,1)}, u32[]{:S(2)}, u32[]{:S(2)}) async-start(bf16[32,256,512]{2,1,0:T(8,128)(2,1)} %select_select_fusion), calls=%async_computation.1 | async-start | bytes 16777216 | tf_op jit(solution)/shard_map/all_to_all | solution.py:91
Sparse Core Ops, SparseCore 0:
  16.4 83.5 reduce-scatter.1
  118.9 47.8 all-gather.1
where the time goes:
time: 309 us
  waiting for transfers between devices  212 us (69%)
  matrix products  26.7 us (9%)
  blocking collectives  19 us (6%)
  other arithmetic  17.5 us (6%)
  between operations  14.3 us (5%)
  local copies, waits for them, and re-layouts  11.7 us (4%)
  starting transfers between devices  7.27 us (2%)
    all_to_all x1, waiting for transfers between devices, body(): lax.all_to_all(pack_rows(result, send_index, send_live), 'grp', split_axi...  105 us
    reduce_scatter x1, waiting for transfers between devices, solve_weights(): lax.psum_scatter(gram_local, 'own', scatter_dimension=0, tiled=True)  59.6 us
    all_gather x1, waiting for transfers between devices, solve_weights(): lax.all_gather(newton_weights(gram_part, right_part), 'own', axis=0, tile...  47.3 us
    unnamed x1, blocking collectives  19 us
    select_n x1, other arithmetic, pack_rows(): return jnp.where(keep_mask, picked, jnp.zeros_like(picked))  7.57 us
    all_to_all x1, starting transfers between devices, body(): lax.all_to_all(pack_rows(result, send_index, send_live), 'grp', split_axi...  7.23 us
    dot_general x1, matrix products, solve_weights(): jnp.einsum('gpk,gpl->gkl', weighted, obs_pert, preferred_element_type=jnp...  6.28 us
  transfers between devices with their start and end apart: 3, of which 3 were waited for; matrix products, arithmetic and copies ran while one was open for 2% of the time, Pallas kernels for 0%

commit v1 on v0

--- a/solution.py
+++ b/solution.py
@@ -4,6 +4,11 @@
 from jax.sharding import PartitionSpec as P
 
 NS_IT = 4
+
+
+def gather_by_exchange(x, axis, dim):
+    copies = jnp.concatenate([x] * lax.axis_size(axis), axis=dim)
+    return lax.all_to_all(copies, axis, dim, dim, tiled=True)
 
 
 def newton_weights(gram, right_side):
@@ -42,7 +47,7 @@
         lax.psum_scatter(gram_local, "own", scatter_dimension=0, tiled=True),
         lax.psum_scatter(right_local, "own", scatter_dimension=0, tiled=True),
     )
-    return lax.all_gather(newton_weights(gram_part, right_part), "own", axis=0, tiled=True)
+    return gather_by_exchange(newton_weights(gram_part, right_part), "own", 0)
 
 
 def apply_weights(state_here, weights):

time: 309 us -> 317 us (1.026)
  starting transfers between devices: 7.27 us -> 12.4 us
    all_to_all x0 -> x1, waiting for transfers between devices: none -> 48.3 us  [gather_by_exchange(): return lax.all_to_all(copies, axis, dim, dim, tiled=True)]
    all_gather x1 -> x0, waiting for transfers between devices: 47.3 us -> none  [solve_weights(): lax.all_gather(newton_weights(gram_part, right_part), 'own', axis=0, tile...]
    all_to_all x0 -> x1, starting transfers between devices: none -> 5.17 us  [gather_by_exchange(): return lax.all_to_all(copies, axis, dim, dim, tiled=True)]
  transfers between devices with their start and end apart: 3 -> 3, of which waited for: 3 -> 3; matrix products, arithmetic and copies ran while one was open for 2% -> 1% of each run, Pallas kernels for 0% -> 0%
where the time goes in v1:
time: 317 us; the launch traced here: 316 us
  waiting for transfers between devices  213 us (67%)
  matrix products  26.7 us (8%)
  blocking collectives  18.9 us (6%)
  other arithmetic  18.8 us (6%)
  between operations  14.3 us (5%)
  starting transfers between devices  12.4 us (4%)
  local copies, waits for them, and re-layouts  11.7 us (4%)
    all_to_all x1, waiting for transfers between devices, body(): lax.all_to_all(pack_rows(result, send_index, send_live), 'grp', split_axi...  105 us
    reduce_scatter x1, waiting for transfers between devices, solve_weights(): lax.psum_scatter(gram_local, 'own', scatter_dimension=0, tiled=True)  59.7 us
    all_to_all x1, waiting for transfers between devices, gather_by_exchange(): return lax.all_to_all(copies, axis, dim, dim, tiled=True)  48.3 us
    unnamed x1, blocking collectives  18.9 us
    select_n x1, other arithmetic, pack_rows(): return jnp.where(keep_mask, picked, jnp.zeros_like(picked))  7.57 us
    all_to_all x1, starting transfers between devices, body(): lax.all_to_all(pack_rows(result, send_index, send_live), 'grp', split_axi...  7.23 us
  transfers between devices with their start and end apart: 3, of which 3 were waited for; matrix products, arithmetic and copies ran while one was open for 1% of the time, Pallas kernels for 0%

profile of v1, /device:TPU:0, one launch (start us, length us, event | category | flops | bytes accessed | tf_op | source)
XLA Modules:
  0.0 316.3 jit_solution(16771104277405262836)
XLA Ops:
  6.5 3.0 convert_reduce_fusion
  10.0 6.3 %fusion.1 = f32[8,512,512]{2,1,0:T(8,128)} fusion(f32[8,512]{1,0:T(8,128)S(1)} %fusion.16, bf16[8,512,512]{2,1,0:T(8,128)(2,1)S(1)} %copy-done, f32[8,512]{1,0:T(8,128)S(1)} %broadcast_multiply_fusion), kind=kOutput, calls=%fused_computation.7 | convolution fusion | flops 2166358016 | bytes 12615680 | tf_op jit(solution)/shard_map/gpk,gpl->gkl/dot_general | solution.py:44
  17.1 2.8 fusion.5
  21.1 18.9 %all-reduce = bf16[8,512]{1,0:T(8,128)(2,1)S(1)} all-reduce(f32[8,512]{1,0:T(8,128)S(1)} %bitcast.53), channel_id=3, replica_groups=mesh['grp'=32,'own'=4] {'own'}, use_global_device_ids=true, to_apply=%region_8.9.clone | all-reduce | flops 4096 | bytes 24576
  40.3 59.7 %reduce-scatter.2.cloned.1.call-done = f32[2,512,512]{2,1,0:T(8,128)} async-done(((f32[8,512,512]{2,1,0:T(8,128)}), f32[2,512,512]{2,1,0:T(8,128)}) %reduce-scatter.2.cloned.1.call-update) | async-done | bytes 2097168 | tf_op jit(solution)/shard_map/reduce_scatter | solution.py:47
  100.0 2.1 multiply_reduce_fusion
  103.5 0.7 convolution_convert_fusion.5
  104.2 0.7 convolution_convert_fusion.6
  105.0 0.7 subtract_convert_fusion.2
  107.1 0.7 subtract_convert_fusion.1
  107.9 1.0 copy-done.8
  108.9 1.7 convolution_convert_fusion.2
  110.5 3.8 %subtract_convert_fusion = bf16[2,512,512]{2,1,0:T(8,128)(2,1)} fusion(bf16[2,512,512]{2,1,0:T(8,128)(2,1)} %convolution_convert_fusion.2, bf16[2,512,512]{2,1,0:T(8,128)(2,1)S(1)} %convolution_convert_fusion.3, bf16[2,512,512]{2,1,0:T(8,128)(2,1)} %copy-done.8, f32[512,512]{1,0:T(8,128)S(1)} %fusion.9), kind=kOutput, calls=%fused_computation.16 | convolution fusion | flops 1075838976 | bytes 5242880 | tf_op jit(solution)/shard_map/gij,gjk->gik/dot_general | solution.py:22
  114.4 2.2 convolution_convert_fusion
  117.8 2.3 pad_maximum_fusion
  120.1 5.2 %all-to-all-start = ((bf16[8,512,512]{2,1,0:T(8,128)(2,1)}), bf16[8,512,512]{2,1,0:T(8,128)(2,1)}, u32[]{:S(2)}, u32[]{:S(2)}) async-start(bf16[8,512,512]{2,1,0:T(8,128)(2,1)} %pad_maximum_fusion), calls=%async_computation.1 | async-start | bytes 8388608 | tf_op jit(solution)/shard_map/all_to_all | solution.py:11
  125.9 48.3 %all-to-all-done = bf16[8,512,512]{2,1,0:T(8,128)(2,1)} async-done(((bf16[8,512,512]{2,1,0:T(8,128)(2,1)}), bf16[8,512,512]{2,1,0:T(8,128)(2,1)}, u32[]{:S(2)}, u32[]{:S(2)}) %all-to-all-start) | async-done | bytes 4194336 | tf_op jit(solution)/shard_map/all_to_all | solution.py:11
  174.2 4.1 %add_convert_fusion = bf16[8,256,512]{2,1,0:T(8,128)(2,1)S(1)} fusion(bf16[8,512,512]{2,1,0:T(8,128)(2,1)} %all-to-all-done, bf16[8,256,512]{2,1,0:T(8,128)(2,1)} %param.6, f32[8,256]{1,0:T(8,128)S(1)} %broadcast_multiply_fusion.1), kind=kOutput, calls=%fused_computation.12 | convolution fusion | flops 1078984704 | bytes 8396800 | tf_op jit(solution)/shard_map/grk,gkl->grl/dot_general | solution.py:56
  178.3 4.8 %gather_fusion = bf16[32,256,512]{2,1,0:T(8,128)(2,1)} fusion(bf16[8,256,512]{2,1,0:T(8,128)(2,1)S(1)} %add_convert_fusion, s32[1024]{0:T(1024)S(1)} %pad_clamp_fusion.1), kind=kCustom, calls=%fused_computation | custom fusion | bytes 16777344 | tf_op jit(solution)/shard_map/jit(_take)/gather | solution.py:63
  183.2 7.6 %select_select_fusion = bf16[32,256,512]{2,1,0:T(8,128)(2,1)} fusion(bf16[32,256,512]{2,1,0:T(8,128)(2,1)} %gather_fusion, pred[32]{0:T(512)(128)(4,1)S(1)} %compare_and_fusion, pred[32]{0:T(512)(128)(4,1)S(1)} %fusion.23), kind=kLoop, calls=%fused_computation.5 | loop fusion | flops 8388608 | bytes 16777280 | tf_op jit(solution)/shard_map/jit(_where)/select_n | solution.py:65
  190.7 7.2 %all-to-all-start.1 = ((bf16[32,256,512]{2,1,0:T(8,128)(2,1)}), bf16[32,256,512]{2,1,0:T(8,128)(2,1)}, u32[]{:S(2)}, u32[]{:S(2)}) async-start(bf16[32,256,512]{2,1,0:T(8,128)(2,1)} %select_select_fusion), calls=%async_computation.2 | async-start | bytes 16777216 | tf_op jit(solution)/shard_map/all_to_all | solution.py:96
  198.3 105.5 %all-to-all-done.1 = bf16[32,256,512]{2,1,0:T(8,128)(2,1)} async-done(((bf16[32,256,512]{2,1,0:T(8,128)(2,1)}), bf16[32,256,512]{2,1,0:T(8,128)(2,1)}, u32[]{:S(2)}, u32[]{:S(2)}) %all-to-all-start.1) | async-done | bytes 8388640 | tf_op jit(solution)/shard_map/all_to_all | solution.py:96
  303.8 4.1 %gather_fusion.1 = bf16[8,256,512]{2,1,0:T(8,128)(2,1)S(1)} fusion(bf16[32,256,512]{2,1,0:T(8,128)(2,1)} %all-to-all-done.1, s32[1024]{0:T(1024)S(1)} %pad_clamp_fusion), kind=kCustom, calls=%fused_computation.1 | custom fusion | bytes 4194336 | tf_op jit(solution)/shard_map/jit(_take)/gather | solution.py:95
  307.9 1.6 broadcast_select_fusion
  (52 shorter events, 7.0 us)
Async XLA Ops:
  6.5 3.0 copy-start.6
  6.5 3.0 copy-start.3
  6.5 93.5 %reduce-scatter.2.cloned.1.call-start = ((), (), s32[]{:S(2)}) async-start(), calls=%async_computation.3 | async-start | bytes 10485760 | tf_op jit(solution)/shard_map/reduce_scatter | solution.py:47
  6.5 3.5 %copy-start = (bf16[8,512,512]{2,1,0:T(8,128)(2,1)S(1)}, bf16[8,512,512]{2,1,0:T(8,128)(2,1)}, u32[]{:S(2)}) copy-start(bf16[8,512,512]{2,1,0:T(8,128)(2,1)} %param.7) | copy-start | bytes 12582916
  16.3 0.7 copy-start.5
  16.3 3.5 %copy-start.7 = (u32[128]{0:T(128)S(1)}, u32[128]{0:T(128)}, u32[]{:S(2)}) copy-start(u32[128]{0:T(128)} %constant.82) | copy-start | bytes 1540
  100.0 2.2 copy-start.1
  107.9 1.0 copy-start.8
  120.1 5.2 %copy-start.4 = (s32[256]{0:T(256)S(1)}, s32[256]{0:T(256)}, u32[]{:S(2)}) copy-start(s32[256]{0:T(256)} %param.11) | copy-start | bytes 3076
  120.1 5.5 %copy-start.2 = (bf16[8,256,512]{2,1,0:T(8,128)(2,1)S(1)}, bf16[8,256,512]{2,1,0:T(8,128)(2,1)}, u32[]{:S(2)}) copy-start(bf16[8,256,512]{2,1,0:T(8,128)(2,1)} %param.6) | copy-start | bytes 6291460
  120.1 54.1 %all-to-all-start = ((bf16[8,512,512]{2,1,0:T(8,128)(2,1)}), bf16[8,512,512]{2,1,0:T(8,128)(2,1)}, u32[]{:S(2)}, u32[]{:S(2)}) async-start(bf16[8,512,512]{2,1,0:T(8,128)(2,1)} %pad_maximum_fusion), calls=%async_computation.1 | async-start | bytes 8388608 | tf_op jit(solution)/shard_map/all_to_all | solution.py:11
  190.7 113.1 %all-to-all-start.1 = ((bf16[32,256,512]{2,1,0:T(8,128)(2,1)}), bf16[32,256,512]{2,1,0:T(8,128)(2,1)}, u32[]{:S(2)}, u32[]{:S(2)}) async-start(bf16[32,256,512]{2,1,0:T(8,128)(2,1)} %select_select_fusion), calls=%async_computation.2 | async-start | bytes 16777216 | tf_op jit(solution)/shard_map/all_to_all | solution.py:96
Sparse Core Ops, SparseCore 0:
  16.4 83.5 reduce-scatter.1
